TPU v7x, 32 devices: a whole 2x2x4 slice. The times are simulated.
32 devices in a mesh: row: 4 (over y, core), col: 8 (over z, x).
Axes of the slice: x: 2, y: 2, z: 4, core: 2. Of those that a mesh axis runs over, the one named last changes fastest.
Arguments:
- node_feats: bfloat16 [8192, 512], P(('row', 'col')), may hold values from -6 to 6
- w_gate: bfloat16 [512, 2048], P(None, ('row', 'col')), may hold values from -0.25 to 0.25
- w_up: bfloat16 [512, 2048], P(None, ('row', 'col')), may hold values from -0.25 to 0.25
- w_down: bfloat16 [2048, 512], P(('row', 'col')), may hold values from -0.125 to 0.125
- tile_src: int32 [512], P(('row', 'col')), may hold values from 0 to 3
- tile_dst: int32 [512], P(('row', 'col')), may hold values from 0 to 1
- tile_mask: int32 [512, 512, 512], P(('row', 'col')), may hold values 0 or 1
- tile_count: int32 [32], P(('row', 'col')), may hold values from 1 to 16, as said below
Outputs:
- entry_loss: float32 [], replicated
- grad_gate: float32 [512, 2048], P(None, ('row', 'col'))
- grad_up: float32 [512, 2048], P(None, ('row', 'col'))
- grad_down: float32 [2048, 512], P(('row', 'col'))
Inputs may be any that keep to these rules, and one draw needn't show every extreme that they name: `tile_count`: some device has all 16 slots live.
All inputs are finite; a program needn't handle non-finite values. No bound on the sum of `tile_mask` on one device may be relied on, other than what follows from the above.
Results may differ from a plain program's by a relative error of at most 0.01.
Values may be sent and summed in bfloat16 or wider, within the bound.
A program may use at most 128 MiB of HBM per device.

v0:
```python
import jax
import jax.numpy as jnp
from jax import lax
from jax.sharding import PartitionSpec as P

BLOCK = 512


def per_device(node_feats, w_gate, w_up, w_down, tile_src, tile_dst, tile_mask, tile_count):
    width = node_feats.shape[1]
    paired = jnp.stack((w_gate, w_up))
    gate_up = jnp.einsum(
        "nd,kdf->knf",
        node_feats,
        lax.all_gather(paired, ("row", "col"), axis=2, tiled=True),
        preferred_element_type=jnp.float32,
    )
    gate_proj = gate_up[0]
    up_proj = gate_up[1]
    hidden = (jax.nn.silu(gate_proj) * up_proj).astype(jnp.bfloat16)
    down_whole = lax.all_gather(w_down, ("row", "col"), axis=0, tiled=True)
    branch_out = jnp.dot(hidden, down_whole, preferred_element_type=jnp.float32)
    embedding = (node_feats.astype(jnp.float32) + branch_out).astype(jnp.bfloat16)
    src_rows = lax.all_gather(embedding, "col", axis=0, tiled=True)
    dst_rows = lax.all_gather(embedding, "row", axis=0, tiled=True)
    tiles_live = lax.psum(tile_count[0].astype(jnp.float32), ("row", "col"))
    score_scale = width ** (-0.5)
    grad_factor = score_scale / tiles_live

    def tile_step(slot, carry):
        loss_part, src_part, dst_part = carry
        src_start = tile_src[slot] * BLOCK
        dst_start = tile_dst[slot] * BLOCK
        src_block = lax.dynamic_slice_in_dim(src_rows, src_start, BLOCK, 0)
        dst_block = lax.dynamic_slice_in_dim(dst_rows, dst_start, BLOCK, 0)
        scores = (
            lax.dot_general(
                src_block, dst_block, (((1,), (1,)), ((), ())), preferred_element_type=jnp.float32
            )
            * score_scale
        )
        labels = lax.dynamic_index_in_dim(tile_mask, slot, 0, keepdims=False).astype(jnp.float32)
        loss_part = loss_part + jnp.sum(jax.nn.softplus(scores) - labels * scores)
        score_grad = ((jax.nn.sigmoid(scores) - labels) * grad_factor).astype(jnp.bfloat16)
        src_term = jnp.dot(score_grad, dst_block, preferred_element_type=jnp.float32)
        dst_term = lax.dot_general(
            score_grad, src_block, (((0,), (0,)), ((), ())), preferred_element_type=jnp.float32
        )
        old_src = lax.dynamic_slice_in_dim(src_part, src_start, BLOCK, 0)
        src_part = lax.dynamic_update_slice_in_dim(src_part, old_src + src_term, src_start, 0)
        old_dst = lax.dynamic_slice_in_dim(dst_part, dst_start, BLOCK, 0)
        dst_part = lax.dynamic_update_slice_in_dim(dst_part, old_dst + dst_term, dst_start, 0)
        return (loss_part, src_part, dst_part)

    start_carry = (
        jnp.zeros((), jnp.float32),
        jnp.zeros(src_rows.shape, jnp.float32),
        jnp.zeros(dst_rows.shape, jnp.float32),
    )
    loss_part, src_part, dst_part = lax.fori_loop(0, tile_count[0], tile_step, start_carry)
    src_grad = lax.psum_scatter(
        src_part.astype(jnp.bfloat16), "col", scatter_dimension=0, tiled=True
    ).astype(jnp.float32)
    dst_grad = lax.psum_scatter(
        dst_part.astype(jnp.bfloat16), "row", scatter_dimension=0, tiled=True
    ).astype(jnp.float32)
    embed_grad = (src_grad + dst_grad).astype(jnp.bfloat16)
    loss_sum = lax.psum(loss_part, ("row", "col"))
    entry_loss = loss_sum / (tiles_live * BLOCK * BLOCK)
    grad_down = lax.psum_scatter(
        lax.dot_general(
            hidden, embed_grad, (((0,), (0,)), ((), ())), preferred_element_type=jnp.float32
        ),
        ("row", "col"),
        scatter_dimension=0,
        tiled=True,
    )
    hidden_grad = lax.dot_general(
        embed_grad, down_whole, (((1,), (1,)), ((), ())), preferred_element_type=jnp.float32
    )
    sig = jax.nn.sigmoid(gate_proj)
    gate_grad = (hidden_grad * up_proj * sig * (1.0 + gate_proj * (1.0 - sig))).astype(jnp.bfloat16)
    up_grad = (hidden_grad * gate_proj * sig).astype(jnp.bfloat16)
    gate_local = lax.dot_general(
        node_feats, gate_grad, (((0,), (0,)), ((), ())), preferred_element_type=jnp.float32
    )
    up_local = lax.dot_general(
        node_feats, up_grad, (((0,), (0,)), ((), ())), preferred_element_type=jnp.float32
    )
    grad_gate, grad_up = (
        lax.psum_scatter(gate_local, ("row", "col"), scatter_dimension=1, tiled=True),
        lax.psum_scatter(up_local, ("row", "col"), scatter_dimension=1, tiled=True),
    )
    return (entry_loss, grad_gate, grad_up, grad_down)


def solution(mesh):
    in_specs = (
        P(("row", "col"), None),
        P(None, ("row", "col")),
        P(None, ("row", "col")),
        P(("row", "col"), None),
        P(("row", "col")),
        P(("row", "col")),
        P(("row", "col"), None, None),
        P(("row", "col")),
    )
    out_specs = (P(), P(None, ("row", "col")), P(None, ("row", "col")), P(("row", "col"), None))
    return jax.shard_map(
        per_device, mesh=mesh, in_specs=in_specs, out_specs=out_specs, check_vma=False
    )
```

profile of v0, /device:TPU:0, one launch (start us, length us, event | category | flops | bytes accessed | tf_op | source)
XLA Modules:
  0.0 938.8 jit_solution(17446640443444854888)
XLA Ops:
  9.6 66.4 %all-gather.5.cloned.1.call-done = bf16[2,512,2048]{1,2,0:T(8,128)(2,1)} async-done(((bf16[2,512,64]{1,2,0:T(8,128)(2,1)}), bf16[2,512,2048]{1,2,0:T(8,128)(2,1)}) %all-gather.5.cloned.1.call-update) | async-done | bytes 4194320 | tf_op jit(solution)/shard_map/all_gather | solution.py:15
  75.9 3.5 convolution_bitcast_fusion
  79.5 1.9 copy-done
  82.1 51.9 %all-gather.7.cloned.1.call-done = bf16[2048,512]{1,0:T(8,128)(2,1)} async-done(((bf16[64,512]{1,0:T(8,128)(2,1)}), bf16[2048,512]{1,0:T(8,128)(2,1)}) %all-gather.7.cloned.1.call-update) | async-done | bytes 2097168 | tf_op jit(solution)/shard_map/all_gather | solution.py:21
  134.0 3.0 fusion.13
  138.4 39.5 %psum.14 = f32[]{:T(128)} all-reduce(f32[]{:T(128)S(6)} %convert_element_type.45), channel_id=1, replica_groups=mesh['row'=4,'col'=8] {'row','col'}, use_global_device_ids=true, to_apply=%region_0.1 | all-reduce | flops 1 | bytes 8 | tf_op jit(solution)/shard_map/psum | solution.py:26
  178.5 26.0 %all-gather.9.cloned.1.call-done = bf16[2048,512]{1,0:T(8,128)(2,1)} async-done(((bf16[256,512]{1,0:T(8,128)(2,1)}), bf16[2048,512]{1,0:T(8,128)(2,1)}) %all-gather.9.cloned.1.call-update) | async-done | bytes 2097168 | tf_op jit(solution)/shard_map/all_gather | solution.py:24
  204.7 2.5 broadcast_in_dim.6
  207.3 190.0 %while.14 = (s32[]{:T(128)}, f32[]{:T(128)}, f32[2048,512]{1,0:T(8,128)}, f32[1024,512]{1,0:T(8,128)S(1)}, s32[]{:T(128)}, /*index=5*/s32[16]{0:T(128)S(1)}, bf1...) while((s32[]{:T(128)}, f32[]{:T(128)}, ...), condition=%wide.region_3.4_spmd, body=%wide.region_1.3_spmd.sunk | while | flops 810287104 | bytes 13108099 | solution.py:60
  210.4 3.7 fusion.41
  214.8 1.6 fusion.43
  216.4 2.7 fusion.42
  222.3 3.7 fusion.41
  226.6 1.6 fusion.43
  228.3 2.7 fusion.42
  234.1 3.7 fusion.41
  238.5 1.6 fusion.43
  240.1 2.7 fusion.42
  246.0 3.7 fusion.41
  250.3 1.6 fusion.43
  252.0 2.7 fusion.42
  257.8 3.7 fusion.41
  262.2 1.6 fusion.43
  263.8 2.6 fusion.42
  269.6 3.7 fusion.41
  274.0 1.6 fusion.43
  275.6 2.6 fusion.42
  281.4 3.7 fusion.41
  285.8 1.6 fusion.43
  287.4 2.7 fusion.42
  293.3 3.7 fusion.41
  297.6 1.6 fusion.43
  299.3 2.7 fusion.42
  305.1 3.7 fusion.41
  309.5 1.6 fusion.43
  311.1 2.6 fusion.42
  316.9 3.7 fusion.41
  321.3 1.6 fusion.43
  322.9 2.7 fusion.42
  328.7 3.7 fusion.41
  334.7 2.6 fusion.42
  340.5 3.7 fusion.41
  344.9 1.6 fusion.43
  346.5 2.7 fusion.42
  352.4 3.7 fusion.41
  358.4 2.7 fusion.42
  364.3 3.7 fusion.41
  368.6 1.6 fusion.43
  370.3 2.7 fusion.42
  376.1 3.7 fusion.41
  380.5 1.6 fusion.43
  382.1 2.7 fusion.42
  388.0 3.7 fusion.41
  394.0 2.6 fusion.42
  398.4 3.8 convert_element_type.46
  402.3 18.3 %reduce-scatter.8.cloned.1.call-done = bf16[256,512]{1,0:T(8,128)(2,1)} async-done(((bf16[1024,512]{1,0:T(8,128)(2,1)}), bf16[256,512]{1,0:T(8,128)(2,1)}) %reduce-scatter.8.cloned.1.call-update) | async-done | bytes 262160 | tf_op jit(solution)/shard_map/reduce_scatter | solution.py:64
  420.6 71.7 %reduce-scatter.6.cloned.1.call-done = bf16[256,512]{1,0:T(8,128)(2,1)} async-done(((bf16[2048,512]{1,0:T(8,128)(2,1)}), bf16[256,512]{1,0:T(8,128)(2,1)}) %reduce-scatter.6.cloned.1.call-update) | async-done | bytes 262160 | tf_op jit(solution)/shard_map/reduce_scatter | solution.py:61
  492.4 3.7 fusion.17
  500.7 2.7 convolution_bitcast_fusion.1
  505.0 5.4 convolution_bitcast_fusion.2
  511.0 42.1 %psum.15 = f32[]{:T(128)} all-reduce(f32[]{:T(128)} %get-tuple-element.64), channel_id=1, replica_groups=mesh['row'=4,'col'=8] {'row','col'}, use_global_device_ids=true, to_apply=%region_4.5 | all-reduce | flops 1 | bytes 8 | tf_op jit(solution)/shard_map/psum | solution.py:68
  553.7 86.9 %reduce-scatter.14.cloned.1.call-done = f32[64,512]{1,0:T(8,128)} async-done(((f32[2048,512]{1,0:T(8,128)}), f32[64,512]{1,0:T(8,128)}) %reduce-scatter.14.cloned.1.call-update) | async-done | bytes 131088 | tf_op jit(solution)/shard_map/reduce_scatter | solution.py:70
  640.6 145.2 %reduce-scatter.12.cloned.1.call-done = f32[512,64]{0,1:T(8,128)} async-done(((f32[512,2048]{0,1:T(8,128)}), f32[512,64]{0,1:T(8,128)}) %reduce-scatter.12.cloned.1.call-update) | async-done | bytes 131088 | tf_op jit(solution)/shard_map/reduce_scatter | solution.py:92
  785.8 145.4 %reduce-scatter.10.cloned.1.call-done = f32[512,64]{0,1:T(8,128)} async-done(((f32[512,2048]{0,1:T(8,128)}), f32[512,64]{0,1:T(8,128)}) %reduce-scatter.10.cloned.1.call-update) | async-done | bytes 131088 | tf_op jit(solution)/shard_map/reduce_scatter | solution.py:91
  (114 shorter events, 35.1 us)
Async XLA Ops:
  7.2 68.8 %all-gather.5.cloned.1.call-start = ((), (), s32[]{:S(2)}) async-start(), calls=%async_computation.5 | async-start | bytes 4325376 | tf_op jit(solution)/shard_map/all_gather | solution.py:15
  8.8 125.3 %all-gather.7.cloned.1.call-start = ((), (), s32[]{:S(2)}) async-start(), calls=%async_computation.6 | async-start | bytes 2162688 | tf_op jit(solution)/shard_map/all_gather | solution.py:21
  9.5 168.9 %all-gather.11.cloned.1.call-start = ((), (), s32[]{:S(2)}) async-start(), calls=%async_computation.8 | async-start | bytes 1310720 | tf_op jit(solution)/shard_map/all_gather | solution.py:25
  79.4 2.0 copy-start
  81.4 52.6 %copy-start.10 = (bf16[256,512]{1,0:T(8,128)(2,1)S(1)}, bf16[256,512]{1,0:T(8,128)(2,1)}, u32[]{:S(2)}) copy-start(bf16[256,512]{1,0:T(8,128)(2,1)} %param.10) | copy-start | bytes 786436
  82.1 55.0 %copy-start.2 = (bf16[256,2048]{0,1:T(8,128)(2,1)}, bf16[256,2048]{0,1:T(8,128)(2,1)S(1)}, u32[]{:S(2)}) copy-start(bf16[256,2048]{0,1:T(8,128)(2,1)S(1)} %multiply_convert_fusion.2) | copy-start | bytes 3145732
  137.1 67.4 %all-gather.9.cloned.1.call-start = ((), (), s32[]{:S(2)}) async-start(), calls=%async_computation.7 | async-start | bytes 2359296 | tf_op jit(solution)/shard_map/all_gather | solution.py:24
  137.7 283.0 %reduce-scatter.8.cloned.1.call-start = ((), (), s32[]{:S(2)}) async-start(), calls=%async_computation.10 | async-start | bytes 1310720 | tf_op jit(solution)/shard_map/reduce_scatter | solution.py:64
  204.7 2.5 copy-start.11
  204.7 2.5 copy-start.12
  214.8 1.7 copy-start.4
  226.6 1.7 copy-start.4
  238.5 1.7 copy-start.4
  250.3 1.7 copy-start.4
  262.2 1.7 copy-start.4
  274.0 1.7 copy-start.4
  285.8 1.7 copy-start.4
  297.6 1.7 copy-start.4
  309.4 1.7 copy-start.4
  321.2 1.7 copy-start.4
  333.1 1.7 copy-start.4
  344.9 1.7 copy-start.4
  356.8 1.7 copy-start.4
  368.6 1.7 copy-start.4
  380.4 1.7 copy-start.4
  392.3 1.7 copy-start.4
  398.4 94.0 %reduce-scatter.6.cloned.1.call-start = ((), (), s32[]{:S(2)}) async-start(), calls=%async_computation.9 | async-start | bytes 2359296 | tf_op jit(solution)/shard_map/reduce_scatter | solution.py:61
  402.2 90.1 %copy-start.3 = (bf16[256,2048]{0,1:T(8,128)(2,1)S(1)}, bf16[256,2048]{0,1:T(8,128)(2,1)}, u32[]{:S(2)}) copy-start(bf16[256,2048]{0,1:T(8,128)(2,1)} %copy-done.2) | copy-start | bytes 3145732
  402.3 238.4 %reduce-scatter.14.cloned.1.call-start = ((), (), s32[]{:S(2)}) async-start(), calls=%async_computation.13 | async-start | bytes 4325376 | tf_op jit(solution)/shard_map/reduce_scatter | solution.py:70
  496.1 1.6 copy-start.5
  496.1 1.6 copy-start.8
  496.1 1.7 copy-start.9
  496.1 289.7 %reduce-scatter.12.cloned.1.call-start = ((), (), s32[]{:S(2)}) async-start(), calls=%async_computation.12 | async-start | bytes 4325376 | tf_op jit(solution)/shard_map/reduce_scatter | solution.py:92
  497.8 2.9 copy-start.1
  498.5 1.3 copy-start.6
  503.4 1.6 copy-start.7
  503.4 427.7 %reduce-scatter.10.cloned.1.call-start = ((), (), s32[]{:S(2)}) async-start(), calls=%async_computation.11 | async-start | bytes 4325376 | tf_op jit(solution)/shard_map/reduce_scatter | solution.py:91
Sparse Core Ops, SparseCore 0:
  11.6 64.3 all-gather.4
  78.9 55.0 all-gather.6
  137.2 15.6 all-gather.10
  154.9 49.5 all-gather.8
  398.5 22.0 reduce-scatter.7
  424.0 68.2 reduce-scatter.5
  496.3 144.3 reduce-scatter.13
  643.5 142.3 reduce-scatter.11
  788.7 142.4 reduce-scatter.9
where the time goes:
time: 942 us; the launch traced here: 939 us
  waiting for transfers between devices  613 us (65%)
  matrix products  147 us (16%)
  blocking collectives  81.5 us (9%)
  loops' own time  43 us (5%)
  local copies, waits for them, and re-layouts  28.9 us (3%)
  between operations  17.5 us (2%)
    reduce_scatter x1, waiting for transfers between devices, per_device(): lax.psum_scatter(gate_local, ('row', 'col'), scatter_dimension=1, tiled=T...  145 us
    reduce_scatter x1, waiting for transfers between devices, per_device(): lax.psum_scatter(up_local, ('row', 'col'), scatter_dimension=1, tiled=True)  145 us
    reduce_scatter x1, waiting for transfers between devices, per_device(): lax.psum_scatter(lax.dot_general(hidden, embed_grad, (((0,), (0,)), ((),...  86.9 us
    reduce_scatter x1, waiting for transfers between devices, per_device(): lax.psum_scatter(src_part.astype(jnp.bfloat16), 'col', scatter_dimension=...  71.7 us
    all_gather x1, waiting for transfers between devices, per_device(): lax.all_gather(paired, ('row', 'col'), axis=2, tiled=True)  66.4 us
    dot_general x16, matrix products, tile_step(): lax.dot_general(src_block, dst_block, (((1,), (1,)), ((), ())), preferred...  59.1 us
    all_gather x1, waiting for transfers between devices, per_device(): down_whole = lax.all_gather(w_down, ('row', 'col'), axis=0, tiled=True)  51.9 us
    another operation x1, loops' own time, per_device(): lax.fori_loop(0, tile_count[0], tile_step, start_carry)  43 us
  transfers between devices with their start and end apart: 9, of which 8 were waited for; matrix products, arithmetic and copies ran while one was open for 2% of the time, Pallas kernels for 0%

commit v1 on v0

v1 whole, which is shorter than its diff:
```python
import functools
import math

import jax
import jax.numpy as jnp
from jax import lax
from jax.experimental import pallas as pl
from jax.experimental.pallas import tpu as pltpu
from jax.sharding import PartitionSpec as P

BLOCK = 512
F32 = jnp.float32
BF16 = jnp.bfloat16
NT = (((1,), (1,)), ((), ()))
TN = (((0,), (0,)), ((), ()))


def dot_nt(a, b):
    return lax.dot_general(a, b, NT, preferred_element_type=F32)


def dot_tn(a, b):
    return lax.dot_general(a, b, TN, preferred_element_type=F32)


def halve(x, op, rows):
    while x.shape[0] > rows:
        half = x.shape[0] // 2
        x = op(x[:half], x[half:])
    return x


def tile_kernel(half_scale, count_ref, src_id, dst_id, src_ref, dst_ref, mask_ref,
                src_out, dst_out, loss_out, src_acc, dst_acc, grad_buf, hinge_acc, log_acc):
    slot = pl.program_id(0)
    width = src_ref.shape[1]

    @pl.when(slot == 0)
    def _():
        src_acc[...] = jnp.zeros_like(src_acc)
        dst_acc[...] = jnp.zeros_like(dst_acc)
        hinge_acc[...] = jnp.zeros_like(hinge_acc)
        log_acc[...] = jnp.zeros_like(log_acc)

    @pl.when(slot < count_ref[0])
    def _():
        src_at = pl.ds(pl.multiple_of(src_id[slot] * BLOCK, BLOCK), BLOCK)
        dst_at = pl.ds(pl.multiple_of(dst_id[slot] * BLOCK, BLOCK), BLOCK)
        dst_block = dst_ref[dst_at, :]
        prods = None
        part = 128
        for lo in range(0, BLOCK, part):
            rows = pl.ds(pl.multiple_of(src_id[slot] * BLOCK + lo, part), part)
            raw = dot_nt(src_ref[rows, :], dst_block)
            sign = jnp.where(mask_ref[0, lo:lo + part, :] == 0, 1.0, -1.0)
            half = jnp.tanh(raw * half_scale)
            grad_buf[lo:lo + part, :] = (half + sign).astype(BF16)
            hinge_acc[...] += halve(jnp.maximum(raw * sign, 0.0), jnp.add, 8)
            prod = halve(1.0 + jnp.abs(half), jnp.multiply, 8)
            prods = prod if prods is None else prods * prod
        log_acc[...] += (BLOCK // 8) * math.log(2.0) - jnp.log(prods)
        grad = grad_buf[...]
        src_acc[src_at, :] += jnp.dot(grad, dst_block, preferred_element_type=F32)
        dst_acc[dst_at, :] += dot_tn(grad, src_ref[src_at, :])

    @pl.when(slot == pl.num_programs(0) - 1)
    def _():
        src_out[...] = src_acc[...].astype(BF16)
        dst_out[...] = dst_acc[...].astype(BF16)
        total = hinge_acc[...] * (2.0 * half_scale) + log_acc[...]
        loss_out[...] = jnp.broadcast_to(jnp.sum(total, keepdims=True), loss_out.shape)


def tiles(src_rows, dst_rows, tile_src, tile_dst, tile_mask, tile_count):
    slots = tile_mask.shape[0]
    width = src_rows.shape[1]
    whole = lambda j, *_: (0, 0)
    return pl.pallas_call(
        functools.partial(tile_kernel, 0.5 * width ** -0.5),
        out_shape=(
            jax.ShapeDtypeStruct(src_rows.shape, BF16),
            jax.ShapeDtypeStruct(dst_rows.shape, BF16),
            jax.ShapeDtypeStruct((8, 128), F32),
        ),
        grid_spec=pltpu.PrefetchScalarGridSpec(
            num_scalar_prefetch=3,
            grid=(slots,),
            in_specs=[
                pl.BlockSpec(src_rows.shape, whole, pipeline_mode=pl.Buffered(1)),
                pl.BlockSpec(dst_rows.shape, whole, pipeline_mode=pl.Buffered(1)),
                pl.BlockSpec((1, BLOCK, BLOCK), lambda j, n, s, d: (jnp.minimum(j, n[0] - 1), 0, 0)),
            ],
            out_specs=[
                pl.BlockSpec(src_rows.shape, whole, pipeline_mode=pl.Buffered(1)),
                pl.BlockSpec(dst_rows.shape, whole, pipeline_mode=pl.Buffered(1)),
                pl.BlockSpec((8, 128), whole),
            ],
            scratch_shapes=[
                pltpu.VMEM(src_rows.shape, F32),
                pltpu.VMEM(dst_rows.shape, F32),
                pltpu.VMEM((BLOCK, BLOCK), BF16),
                pltpu.VMEM((8, BLOCK), F32),
                pltpu.VMEM((8, BLOCK), F32),
            ],
        ),
        compiler_params=pltpu.CompilerParams(vmem_limit_bytes=48 << 20),
        name="tiles",
    )(tile_count, tile_src, tile_dst, src_rows, dst_rows, tile_mask)


def per_device(node_feats, w_gate, w_up, w_down, tile_src, tile_dst, tile_mask, tile_count):
    width = node_feats.shape[1]
    stacked = jnp.stack((w_gate.T, w_up.T, w_down))
    weights = lax.all_gather(stacked, "col", axis=1, tiled=True)
    feats = lax.all_gather(node_feats, "row", axis=0, tiled=True)
    gate_proj = dot_nt(feats, weights[0])
    up_proj = dot_nt(feats, weights[1])
    hidden = (jax.nn.silu(gate_proj) * up_proj).astype(BF16)
    branch = jnp.dot(hidden, weights[2], preferred_element_type=F32).astype(BF16)
    branch_out = lax.psum_scatter(branch, "row", scatter_dimension=0, tiled=True)
    embedding = (node_feats.astype(F32) + branch_out.astype(F32)).astype(BF16)
    src_rows = lax.all_gather(embedding, "col", axis=0, tiled=True)
    dst_rows = lax.all_gather(embedding, "row", axis=0, tiled=True)
    src_part, dst_part, loss_part = tiles(src_rows, dst_rows, tile_src, tile_dst, tile_mask, tile_count)
    src_grad = lax.psum_scatter(src_part, "col", scatter_dimension=0, tiled=True)
    dst_grad = lax.psum_scatter(dst_part, "row", scatter_dimension=0, tiled=True)
    own_grad = (src_grad.astype(F32) + dst_grad.astype(F32)).astype(BF16)
    totals = lax.psum(jnp.stack((loss_part[0, 0], tile_count[0].astype(F32))), ("row", "col"))
    embed_grad = lax.all_gather(own_grad, "row", axis=0, tiled=True)
    hidden_grad = dot_nt(embed_grad, weights[2])
    sig = jax.nn.sigmoid(gate_proj)
    gate_grad = (hidden_grad * up_proj * sig * (1.0 + gate_proj * (1.0 - sig))).astype(BF16)
    up_grad = (hidden_grad * gate_proj * sig).astype(BF16)
    partial = jnp.stack(
        (dot_tn(gate_grad, feats).astype(BF16), dot_tn(up_grad, feats).astype(BF16), dot_tn(hidden, embed_grad).astype(BF16))
    )
    summed = lax.psum_scatter(partial, "col", scatter_dimension=1, tiled=True).astype(F32)
    summed = summed * (0.5 * width ** -0.5 / totals[1])
    entry_loss = totals[0] / (totals[1] * BLOCK * BLOCK)
    return (entry_loss, summed[0].T, summed[1].T, summed[2])


def solution(mesh):
    both = ("row", "col")
    in_specs = (
        P(both, None),
        P(None, both),
        P(None, both),
        P(both, None),
        P(both),
        P(both),
        P(both, None, None),
        P(both),
    )
    out_specs = (P(), P(None, both), P(None, both), P(both, None))
    return jax.shard_map(per_device, mesh=mesh, in_specs=in_specs, out_specs=out_specs, check_vma=False)
```

time: 942 us -> 402 us (0.43)
  waiting for transfers between devices: 613 us -> 292 us
  matrix products: 147 us -> 10.8 us
  loops' own time: 43 us -> 0 us
  blocking collectives: 81.5 us -> 39.6 us
  Pallas kernels: 0 us -> 28.4 us
  local copies, waits for them, and re-layouts: 28.9 us -> 5 us
    reduce_scatter x5 -> x4, waiting for transfers between devices: 467 us -> 142 us  [the longest x1 71.9 us: per_device(): lax.psum_scatter(src_part, 'col', scatter_dimension=0, tiled=True)]
    dot_general x54 -> x7, matrix products: 147 us -> 10.8 us  [the longest x3 6.63 us: dot_nt(): return lax.dot_general(a, b, NT, preferred_element_type=F32)]
    another operation x1 -> x0, loops' own time: 43 us -> none  [per_device(): lax.fori_loop(0, tile_count[0], tile_step, start_carry)]
    psum x2 -> x1, blocking collectives: 81.5 us -> 39.6 us  [per_device(): lax.psum(jnp.stack((loss_part[0, 0], tile_count[0].astype(F32))), ('row',...]
    all_gather x2 -> x3, waiting for transfers between devices: 118 us -> 81.6 us  [the longest x1 46.4 us: per_device(): weights = lax.all_gather(stacked, 'col', axis=1, tiled=True)]
    pallas_call x0 -> x1, Pallas kernels: none -> 28.4 us  [tiles(): pl.pallas_call(functools.partial(tile_kernel, 0.5 * width ** (-0.5)), out...]
    all_gather x1, waiting for transfers between devices: 26 us -> 51.1 us  [per_device(): src_rows = lax.all_gather(embedding, 'col', axis=0, tiled=True)]
    dynamic_slice x32 -> x0, local copies, waits for them, and re-layouts: 18.8 us -> none  [the longest x16 9.41 us: tile_step(): dst_start = tile_dst[slot] * BLOCK]
  transfers between devices with their start and end apart: 9 -> 9, of which waited for: 8 -> 9; matrix products, arithmetic and copies ran while one was open for 2% -> 1% of each run, Pallas kernels for 0% -> 0%
where the time goes in v1:
time: 402 us
  waiting for transfers between devices  292 us (73%)
  blocking collectives  39.6 us (10%)
  Pallas kernels  28.4 us (7%)
  between operations  17.7 us (4%)
  matrix products  10.8 us (3%)
  other arithmetic  8.16 us (2%)
  local copies, waits for them, and re-layouts  5 us (1%)
    reduce_scatter x1, waiting for transfers between devices, per_device(): lax.psum_scatter(src_part, 'col', scatter_dimension=0, tiled=True)  71.9 us
    all_gather x1, waiting for transfers between devices, per_device(): src_rows = lax.all_gather(embedding, 'col', axis=0, tiled=True)  51.1 us
    all_gather x1, waiting for transfers between devices, per_device(): weights = lax.all_gather(stacked, 'col', axis=1, tiled=True)  46.4 us
    psum x1, blocking collectives, per_device(): lax.psum(jnp.stack((loss_part[0, 0], tile_count[0].astype(F32))), ('row',...  39.6 us
    pallas_call x1, Pallas kernels, tiles(): pl.pallas_call(functools.partial(tile_kernel, 0.5 * width ** (-0.5)), out...  28.4 us
    reduce_scatter x1, waiting for transfers between devices, per_device(): lax.psum_scatter(partial, 'col', scatter_dimension=1, tiled=True)  23.9 us
    reduce_scatter x1, waiting for transfers between devices, per_device(): lax.psum_scatter(branch, 'row', scatter_dimension=0, tiled=True)  23.3 us
    reduce_scatter x1, waiting for transfers between devices, per_device(): lax.psum_scatter(dst_part, 'row', scatter_dimension=0, tiled=True)  22.7 us
  transfers between devices with their start and end apart: 9, of which 9 were waited for; matrix products, arithmetic and copies ran while one was open for 1% of the time, Pallas kernels for 0%

profile of v1, /device:TPU:0, one launch (start us, length us, event | category | flops | bytes accessed | tf_op | source)
XLA Modules:
  0.0 402.1 jit_solution(8737312721177894311)
XLA Ops:
  7.2 0.0 all-gather.8.cloned.1.call-start
  7.2 0.7 all-gather.8.cloned.1.call-update
  7.9 0.0 all-gather.6.cloned.1.call-start
  7.9 1.6 pad_maximum_fusion.1
  9.5 0.0 all-gather.6.cloned.1.call-update
  9.6 0.0 reduce-scatter.5.cloned.1.call-start
  9.6 19.4 %all-gather.8.cloned.1.call-done = bf16[1024,512]{1,0:T(8,128)(2,1)} async-done(((bf16[256,512]{1,0:T(8,128)(2,1)}), bf16[1024,512]{1,0:T(8,128)(2,1)}) %all-gather.8.cloned.1.call-update) | async-done | bytes 1048592 | tf_op jit(solution)/shard_map/all_gather | solution.py:115
  29.0 0.0 copy-start.3
  29.0 46.4 %all-gather.6.cloned.1.call-done = bf16[3,512,512]{2,1,0:T(8,128)(2,1)} async-done(((bf16[3,64,512]{2,1,0:T(8,128)(2,1)}), bf16[3,512,512]{2,1,0:T(8,128)(2,1)}) %all-gather.6.cloned.1.call-update) | async-done | bytes 1572880 | tf_op jit(solution)/shard_map/all_gather | solution.py:114
  75.4 0.0 copy-start.6
  75.4 2.2 fusion.16
  77.6 0.0 copy-done.3
  77.6 0.0 copy-done.6
  77.7 2.2 fusion
  79.8 0.0 copy-start.7
  79.8 1.0 copy-done.7
  80.9 0.0 copy-start.5
  80.9 0.0 copy-start.1
  80.9 1.7 convolution_convert_fusion
  82.6 0.0 reduce-scatter.5.cloned.1.call-update
  82.6 0.0 all-gather.12.cloned.1.call-start
  82.7 23.3 %reduce-scatter.5.cloned.1.call-done = bf16[256,512]{1,0:T(8,128)(2,1)} async-done(((bf16[1024,512]{1,0:T(8,128)(2,1)}), bf16[256,512]{1,0:T(8,128)(2,1)}) %reduce-scatter.5.cloned.1.call-update) | async-done | bytes 262160 | tf_op jit(solution)/shard_map/reduce_scatter | solution.py:120
  105.9 0.0 copy-done.5
  105.9 1.7 add_convert_fusion.1
  107.7 0.0 all-gather.12.cloned.1.call-update
  107.7 0.0 all-gather.10.cloned.1.call-start
  107.7 0.5 all-gather.10.cloned.1.call-update
  108.3 0.0 reduce-scatter.9.cloned.1.call-start
  109.0 15.6 %all-gather.12.cloned.1.call-done.dst_ref = bf16[1024,512]{1,0:T(8,128)(2,1)} async-done(((bf16[256,512]{1,0:T(8,128)(2,1)}), bf16[1024,512]{1,0:T(8,128)(2,1)}) %all-gather.12.cloned.1.call-update) | async-done | bytes 1048592 | tf_op jit(solution)/shard_map/all_gather | solution.py:123
  124.5 51.1 %all-gather.10.cloned.1.call-done.src_ref = bf16[2048,512]{1,0:T(8,128)(2,1)} async-done(((bf16[256,512]{1,0:T(8,128)(2,1)}), bf16[2048,512]{1,0:T(8,128)(2,1)}) %all-gather.10.cloned.1.call-update) | async-done | bytes 2097168 | tf_op jit(solution)/shard_map/all_gather | solution.py:122
  175.6 0.0 copy-done.1
  175.6 0.0 copy-done.2
  175.6 0.0 copy-start
  175.6 1.2 copy-done
  176.9 28.4 %tiles.1 = (bf16[2048,512]{1,0:T(8,128)(2,1)}, bf16[1024,512]{1,0:T(8,128)(2,1)}, f32[8,128]{1,0:T(8,128)S(1)}) custom-call(s32[1]{0:T(128)S(6)} %copy.15.count_ref, s32[16]{0:T(128)S(1)} %copy-done.1, s32[16]{0:T(128)S(1)} %copy-done.2, bf16[2048,512]{1,0:T(8,128)(2,1)} %all-gather.10.cloned.1.call-done.src_ref, bf16[1024,512]{1,0:T(8,128)(2,1)S(1)} %copy-done, ...), custom_call_target="tpu_custom_call" | custom-call | tf_op jit(solution)/shard_map/tiles/pallas_call | solution.py:78
  205.3 0.0 reduce-scatter.9.cloned.1.call-update
  205.3 0.0 reduce-scatter.7.cloned.1.call-start
  205.4 0.7 reduce-scatter.7.cloned.1.call-update
  206.1 0.0 all-gather.14.cloned.1.call-start
  206.1 22.7 %reduce-scatter.9.cloned.1.call-done = bf16[256,512]{1,0:T(8,128)(2,1)} async-done(((bf16[1024,512]{1,0:T(8,128)(2,1)}), bf16[256,512]{1,0:T(8,128)(2,1)}) %reduce-scatter.9.cloned.1.call-update) | async-done | bytes 262160 | tf_op jit(solution)/shard_map/reduce_scatter | solution.py:126
  228.8 71.9 %reduce-scatter.7.cloned.1.call-done = bf16[256,512]{1,0:T(8,128)(2,1)} async-done(((bf16[2048,512]{1,0:T(8,128)(2,1)}), bf16[256,512]{1,0:T(8,128)(2,1)}) %reduce-scatter.7.cloned.1.call-update) | async-done | bytes 262160 | tf_op jit(solution)/shard_map/reduce_scatter | solution.py:125
  300.7 1.8 add_convert_fusion
  302.5 0.0 all-gather.14.cloned.1.call-update
  302.5 0.0 reduce-scatter.11.cloned.1.call-start
  302.6 15.9 %all-gather.14.cloned.1.call-done = bf16[1024,512]{1,0:T(8,128)(2,1)} async-done(((bf16[256,512]{1,0:T(8,128)(2,1)}), bf16[1024,512]{1,0:T(8,128)(2,1)}) %all-gather.14.cloned.1.call-update) | async-done | bytes 1048592 | tf_op jit(solution)/shard_map/all_gather | solution.py:129
  318.4 0.0 copy-start.4
  318.4 0.0 copy-start.8
  318.4 2.2 fusion.17
  320.7 0.0 copy-done.4
  320.7 0.0 copy-done.8
  320.7 0.7 fusion.12
  321.4 0.0 copy-start.9
  321.4 0.7 fusion.11
  322.1 0.9 copy-done.9
  323.0 1.1 fusion.10
  324.1 1.4 pad_maximum_fusion
  325.4 0.0 reduce-scatter.11.cloned.1.call-update
  325.4 0.5 slice.32
  326.0 0.7 pad_maximum_fusion.2
  326.7 39.6 %psum.7 = f32[2]{0:T(128)S(1)} all-reduce(f32[2]{0:T(128)S(1)} %pad_maximum_fusion.2), channel_id=1, replica_groups=mesh['row'=4,'col'=8] {'row','col'}, use_global_device_ids=true, to_apply=%region_1.2 | all-reduce | flops 2 | bytes 16 | tf_op jit(solution)/shard_map/psum | solution.py:128
  366.2 0.6 fusion.20
  368.8 23.9 %reduce-scatter.11.cloned.1.call-done = bf16[3,64,512]{2,1,0:T(8,128)(2,1)} async-done(((bf16[3,512,512]{2,1,0:T(8,128)(2,1)}), bf16[3,64,512]{2,1,0:T(8,128)(2,1)}) %reduce-scatter.11.cloned.1.call-update) | async-done | bytes 196624 | tf_op jit(solution)/shard_map/reduce_scatter | solution.py:137
  392.7 1.0 convert_multiply_fusion
  393.7 0.8 slice_bitcast_fusion.7
  (1 shorter events, 0.0 us)
Async XLA Ops:
  7.2 21.8 %all-gather.8.cloned.1.call-start = ((), (), s32[]{:S(2)}) async-start(), calls=%async_computation.5 | async-start | bytes 1310720 | tf_op jit(solution)/shard_map/all_gather | solution.py:115
  7.9 67.5 %all-gather.6.cloned.1.call-start = ((), (), s32[]{:S(2)}) async-start(), calls=%async_computation.4 | async-start | bytes 1769472 | tf_op jit(solution)/shard_map/all_gather | solution.py:114
  9.6 96.4 %reduce-scatter.5.cloned.1.call-start = ((), (), s32[]{:S(2)}) async-start(), calls=%async_computation.6 | async-start | bytes 1310720 | tf_op jit(solution)/shard_map/reduce_scatter | solution.py:120
  29.0 48.6 %copy-start.3 = (bf16[1024,512]{1,0:T(8,128)(2,1)S(1)}, bf16[1024,512]{1,0:T(8,128)(2,1)}, u32[]{:S(2)}) copy-start(bf16[1024,512]{1,0:T(8,128)(2,1)} %all-gather.8.cloned.1.call-done) | copy-start | bytes 3145732
  75.4 2.3 copy-start.6
  79.8 1.0 copy-start.7
  80.9 25.1 %copy-start.5 = (bf16[256,512]{1,0:T(8,128)(2,1)S(1)}, bf16[256,512]{1,0:T(8,128)(2,1)}, u32[]{:S(2)}) copy-start(bf16[256,512]{1,0:T(8,128)(2,1)} %param.8) | copy-start | bytes 786436
  80.9 94.8 %copy-start.1 = (s32[16]{0:T(128)S(1)}, s32[16]{0:T(128)}, u32[]{:S(2)}) copy-start(s32[16]{0:T(128)} %src_id.1) | copy-start | bytes 196
  80.9 94.8 %copy-start.2 = (s32[16]{0:T(128)S(1)}, s32[16]{0:T(128)}, u32[]{:S(2)}) copy-start(s32[16]{0:T(128)} %dst_id.1) | copy-start | bytes 196
  82.6 41.9 %all-gather.12.cloned.1.call-start = ((), (), s32[]{:S(2)}) async-start(), calls=%async_computation.8 | async-start | bytes 1310720 | tf_op jit(solution)/shard_map/all_gather | solution.py:123
  107.7 67.9 %all-gather.10.cloned.1.call-start = ((), (), s32[]{:S(2)}) async-start(), calls=%async_computation.7 | async-start | bytes 2359296 | tf_op jit(solution)/shard_map/all_gather | solution.py:122
  108.3 120.5 %reduce-scatter.9.cloned.1.call-start = ((), (), s32[]{:S(2)}) async-start(), calls=%async_computation.10 | async-start | bytes 1310720 | tf_op jit(solution)/shard_map/reduce_scatter | solution.py:126
  175.6 1.2 copy-start
  205.3 95.4 %reduce-scatter.7.cloned.1.call-start = ((), (), s32[]{:S(2)}) async-start(), calls=%async_computation.9 | async-start | bytes 2359296 | tf_op jit(solution)/shard_map/reduce_scatter | solution.py:125
  206.1 112.4 %all-gather.14.cloned.1.call-start = ((), (), s32[]{:S(2)}) async-start(), calls=%async_computation.11 | async-start | bytes 1310720 | tf_op jit(solution)/shard_map/all_gather | solution.py:129
  302.5 90.2 %reduce-scatter.11.cloned.1.call-start = ((), (), s32[]{:S(2)}) async-start(), calls=%async_computation.12 | async-start | bytes 1769472 | tf_op jit(solution)/shard_map/reduce_scatter | solution.py:137
  318.4 2.3 copy-start.4
  318.4 2.3 copy-start.8
  321.4 1.6 copy-start.9
Sparse Core Ops, SparseCore 0:
  9.5 19.4 all-gather.7
  31.2 44.1 all-gather.5
  82.7 23.1 reduce-scatter.4
  107.8 16.6 all-gather.11
  126.5 49.0 all-gather.9
  205.4 23.2 reduce-scatter.8
  232.3 68.3 reduce-scatter.6
  302.6 15.7 all-gather.13
  325.6 67.1 reduce-scatter.10

commit v2 on v1

--- a/solution.py
+++ b/solution.py
@@ -108,25 +108,323 @@
     )(tile_count, tile_src, tile_dst, src_rows, dst_rows, tile_mask)
 
 
-def per_device(node_feats, w_gate, w_up, w_down, tile_src, tile_dst, tile_mask, tile_count):
-    width = node_feats.shape[1]
+def finish(steps):
+    steps = list(steps)
+    while steps:
+        steps = [step for step in steps if next(step, True) is None]
+
+
+def group(axis, n, inner):
+    me = lax.axis_index(axis)
+    return me, me // inner, lax.rem(me, inner)
+
+
+def gather(axis, n, inner, src, place, send, recv):
+    outer = n // inner
+    me, at_o, at_i = group(axis, n, inner)
+
+    def line(way, k):
+        block = at_o - k if way == 0 else at_o + k
+        ahead = me + inner if way == 0 else me - inner
+        index = way * (outer - 1) + k
+        return pltpu.make_async_remote_copy(
+            src_ref=src if k == 0 else place(block * inner + at_i),
+            dst_ref=place(me if k == 0 else block * inner + at_i),
+            send_sem=send.at[index],
+            recv_sem=recv.at[index],
+            device_id={axis: ahead},
+        )
+
+    def sends(way, k):
+        if way == 0:
+            return jnp.logical_and(at_o - k >= 0, at_o < outer - 1)
+        return jnp.logical_and(at_o + k < outer, at_o > 0)
+
+    def arrived(way, k):
+        block = at_o - 1 - k if way == 0 else at_o + 1 + k
+        index = way * (outer - 1) + k
+        here = place(block * inner + at_i)
+        return pltpu.make_async_remote_copy(
+            src_ref=here, dst_ref=here, send_sem=send.at[index], recv_sem=recv.at[index], device_id={axis: me}
+        )
+
+    def arrives(way, k):
+        return at_o - 1 - k >= 0 if way == 0 else at_o + 1 + k < outer
+
+    def across(j, block, slot, own, incoming=False):
+        index = 2 * (outer - 1) + (j - 1) * (2 * outer - 1) + slot
+        peer = at_o * inner + lax.rem(at_i + j, inner)
+        where = place(block * inner + (lax.rem(at_i + inner - j, inner) if incoming else at_i))
+        return pltpu.make_async_remote_copy(
+            src_ref=src if own else where,
+            dst_ref=where,
+            send_sem=send.at[index],
+            recv_sem=recv.at[index],
+            device_id={axis: peer},
+        )
+
+    def slots():
+        for way in range(2):
+            for k in range(outer - 1):
+                yield way, k, (at_o - 1 - k if way == 0 else at_o + 1 + k), 1 + way * (outer - 1) + k
+
+    for way in range(2):
+        @pl.when(sends(way, 0))
+        def _(way=way):
+            line(way, 0).start()
+    for j in range(1, inner):
+        across(j, at_o, 0, True).start()
+    here = place(me)
+    here[...] = src[...]
+    yield
+    for step in range(outer - 1):
+        for way, k, block, slot in slots():
+            if k != step:
+                continue
+
+            @pl.when(arrives(way, k))
+            def _(way=way, k=k, block=block, slot=slot):
+                arrived(way, k).wait_recv()
+                for j in range(1, inner):
+                    across(j, block, slot, False).start()
+                if k + 1 < outer - 1:
+                    @pl.when(sends(way, k + 1))
+                    def _():
+                        line(way, k + 1).start()
+        yield
+    for j in range(1, inner):
+        across(j, at_o, 0, True, True).wait_recv()
+        across(j, at_o, 0, True).wait_send()
+    for way, k, block, slot in slots():
+        @pl.when(arrives(way, k))
+        def _(block=block, slot=slot):
+            for j in range(1, inner):
+                across(j, block, slot, False, True).wait_recv()
+                across(j, block, slot, False).wait_send()
+
+        @pl.when(sends(way, k))
+        def _(way=way, k=k):
+            line(way, k).wait_send()
+
+
+def gather_sems(n, inner):
+    outer = n // inner
+    count = 2 * (outer - 1) + (inner - 1) * (2 * outer - 1)
+    return [pltpu.SemaphoreType.DMA((count,)), pltpu.SemaphoreType.DMA((count,))]
+
+
+def reduce(axis, n, inner, place, near, out, far, send, recv, result):
+    outer = n // inner
+    me, at_o, at_i = group(axis, n, inner)
+    order = sorted(range(outer), key=lambda off: -min(off, outer - off))
+
+    def across(j, off):
+        index = (j - 1) * outer + off
+        block = lax.rem(at_o + off, outer) * inner + lax.rem(at_i + j, inner)
+        return pltpu.make_async_remote_copy(
+            src_ref=place(block),
+            dst_ref=near.at[index],
+            send_sem=send.at[index],
+            recv_sem=recv.at[index],
+            device_id={axis: at_o * inner + lax.rem(at_i + j, inner)},
+        )
+
+    def along(off):
+        index = (inner - 1) * outer + off - 1
+        return pltpu.make_async_remote_copy(
+            src_ref=out.at[off - 1],
+            dst_ref=far.at[off - 1],
+            send_sem=send.at[index],
+            recv_sem=recv.at[index],
+            device_id={axis: lax.rem(at_o + off, outer) * inner + at_i},
+        )
+
+    for off in order:
+        for j in range(1, inner):
+            across(j, off).start()
+    yield
+    for off in order:
+        total = place(lax.rem(at_o + off, outer) * inner + at_i)[...].astype(F32)
+        for j in range(1, inner):
+            across(j, off).wait_recv()
+            total = total + near[(j - 1) * outer + off].astype(F32)
+        if off:
+            out[off - 1] = total.astype(BF16)
+            along(off).start()
+            yield
+    for off in order[:-1]:
+        along(off).wait_recv()
+        total = total + far[off - 1].astype(F32)
+    result.append(total)
+    for off in order:
+        for j in range(1, inner):
+            across(j, off).wait_send()
+        if off:
+            along(off).wait_send()
+
+
+def reduce_scratch(n, inner, block):
+    outer = n // inner
+    count = (inner - 1) * outer + outer - 1
+    return [
+        pltpu.VMEM(((inner - 1) * outer,) + block, BF16),
+        pltpu.VMEM((outer - 1,) + block, BF16),
+        pltpu.VMEM((outer - 1,) + block, BF16),
+        pltpu.SemaphoreType.DMA((count,)),
+        pltpu.SemaphoreType.DMA((count,)),
+    ]
+
+
+def sum_over(axis, n, src, slots, send, recv, result):
+    me = lax.axis_index(axis)
+
+    def copy(j):
+        return pltpu.make_async_remote_copy(
+            src_ref=src,
+            dst_ref=slots.at[j - 1],
+            send_sem=send.at[j - 1],
+            recv_sem=recv.at[j - 1],
+            device_id={axis: lax.rem(me + j, n)},
+        )
+
+    for j in range(1, n):
+        copy(j).start()
+    yield
+    total = src[...]
+    for j in range(1, n):
+        copy(j).wait_recv()
+        total = total + slots[j - 1]
+    result.append(total)
+    for j in range(1, n):
+        copy(j).wait_send()
+
+
+def sum_scratch(n):
+    return [
+        pltpu.VMEM((n - 1, 8, 128), F32),
+        pltpu.SemaphoreType.DMA((n - 1,)),
+        pltpu.SemaphoreType.DMA((n - 1,)),
+    ]
+
+
+def greet(axes):
+    barrier = pltpu.get_barrier_semaphore()
+    total = 0
+    for axis, n in axes:
+        me = lax.axis_index(axis)
+        for j in range(1, n):
+            pl.semaphore_signal(barrier, inc=1, device_id={axis: lax.rem(me + j, n)})
+        total += n - 1
+    pl.semaphore_wait(barrier, total)
+
+
+def rows_of(ref, size):
+    return lambda block: ref.at[pl.ds(pl.multiple_of(block * size, size), size), :]
+
+
+def units_of(ref, size):
+    return lambda block: ref.at[:, pl.ds(pl.multiple_of(block * size, size), size), :]
+
+
+def gather_in_kernel(row, col, w_ref, x_ref, w_out, x_out, *sems):
+    greet((("row", row[0]), ("col", col[0])))
+    finish((
+        gather("col", *col, w_ref, units_of(w_out, w_ref.shape[1]), *sems[:2]),
+        gather("row", *row, x_ref, rows_of(x_out, x_ref.shape[0]), *sems[2:]),
+    ))
+
+
+def embed_kernel(row, col, branch_ref, x_ref, src_out, dst_out, held, *scratch):
+    greet((("row", row[0]), ("col", col[0])))
+    size = x_ref.shape[0]
+    branch = []
+    finish((reduce("row", *row, rows_of(branch_ref, size), *scratch[:5], branch),))
+    held[...] = (x_ref[...].astype(F32) + branch[0]).astype(BF16)
+    finish((
+        gather("col", *col, held, rows_of(src_out, size), *scratch[5:7]),
+        gather("row", *row, held, rows_of(dst_out, size), *scratch[7:9]),
+    ))
+
+
+def grad_kernel(row, col, src_ref, dst_ref, tot_ref, grad_out, tot_out, held, tot_held, *scratch):
+    greet((("row", row[0]), ("col", col[0])))
+    size = held.shape[0]
+    own, first, second = [], [], []
+
+    def totals():
+        yield from sum_over("row", row[0], tot_ref, *scratch[12:15], first)
+        tot_held[...] = first[0]
+        yield
+        yield from sum_over("col", col[0], tot_held, *scratch[15:18], second)
+        tot_out[...] = second[0]
+
+    finish((
+        reduce("col", *col, rows_of(src_ref, size), *scratch[:5], own),
+        reduce("row", *row, rows_of(dst_ref, size), *scratch[5:10], own),
+        totals(),
+    ))
+    held[...] = (own[0] + own[1]).astype(BF16)
+    finish((gather("row", *row, held, rows_of(grad_out, size), *scratch[10:12]),))
+
+
+def weight_kernel(col, part_ref, sum_out, *scratch):
+    greet((("col", col[0]),))
+    total = []
+    finish((reduce("col", *col, units_of(part_ref, sum_out.shape[1]), *scratch, total),))
+    sum_out[...] = total[0]
+
+
+def remote(kernel, name, number, outs, scratch):
+    vmem = pl.BlockSpec(memory_space=pltpu.VMEM)
+    return pl.pallas_call(
+        kernel,
+        out_shape=outs,
+        out_specs=jax.tree.map(lambda _: vmem, outs),
+        scratch_shapes=scratch,
+        compiler_params=pltpu.CompilerParams(
+            collective_id=number, has_side_effects=True, vmem_limit_bytes=32 << 20
+        ),
+        name=name,
+    )
+
+
+def per_device(row, col, node_feats, w_gate, w_up, w_down, tile_src, tile_dst, tile_mask, tile_count):
+    size, width = node_feats.shape
+    units = w_down.shape[0]
+    shaped = jax.ShapeDtypeStruct
+    src_shape = shaped((col[0] * size, width), BF16)
+    dst_shape = shaped((row[0] * size, width), BF16)
     stacked = jnp.stack((w_gate.T, w_up.T, w_down))
-    weights = lax.all_gather(stacked, "col", axis=1, tiled=True)
-    feats = lax.all_gather(node_feats, "row", axis=0, tiled=True)
+    weights, feats = remote(
+        functools.partial(gather_in_kernel, row, col),
+        "gather_in",
+        0,
+        (shaped((3, col[0] * units, width), BF16), dst_shape),
+        gather_sems(*col) + gather_sems(*row),
+    )(stacked, node_feats)
     gate_proj = dot_nt(feats, weights[0])
     up_proj = dot_nt(feats, weights[1])
     hidden = (jax.nn.silu(gate_proj) * up_proj).astype(BF16)
     branch = jnp.dot(hidden, weights[2], preferred_element_type=F32).astype(BF16)
-    branch_out = lax.psum_scatter(branch, "row", scatter_dimension=0, tiled=True)
-    embedding = (node_feats.astype(F32) + branch_out.astype(F32)).astype(BF16)
-    src_rows = lax.all_gather(embedding, "col", axis=0, tiled=True)
-    dst_rows = lax.all_gather(embedding, "row", axis=0, tiled=True)
+    src_rows, dst_rows = remote(
+        functools.partial(embed_kernel, row, col),
+        "embed",
+        1,
+        (src_shape, dst_shape),
+        [pltpu.VMEM((size, width), BF16)]
+        + reduce_scratch(*row, (size, width)) + gather_sems(*col) + gather_sems(*row),
+    )(branch, node_feats)
     src_part, dst_part, loss_part = tiles(src_rows, dst_rows, tile_src, tile_dst, tile_mask, tile_count)
-    src_grad = lax.psum_scatter(src_part, "col", scatter_dimension=0, tiled=True)
-    dst_grad = lax.psum_scatter(dst_part, "row", scatter_dimension=0, tiled=True)
-    own_grad = (src_grad.astype(F32) + dst_grad.astype(F32)).astype(BF16)
-    totals = lax.psum(jnp.stack((loss_part[0, 0], tile_count[0].astype(F32))), ("row", "col"))
-    embed_grad = lax.all_gather(own_grad, "row", axis=0, tiled=True)
+    is_loss = lax.broadcasted_iota(jnp.int32, loss_part.shape, 0) == 0
+    embed_grad, totals = remote(
+        functools.partial(grad_kernel, row, col),
+        "grad",
+        2,
+        (dst_shape, shaped(loss_part.shape, F32)),
+        [pltpu.VMEM((size, width), BF16), pltpu.VMEM(loss_part.shape, F32)]
+        + reduce_scratch(*col, (size, width)) + reduce_scratch(*row, (size, width)) + gather_sems(*row)
+        + sum_scratch(row[0]) + sum_scratch(col[0]),
+    )(src_part, dst_part, jnp.where(is_loss, loss_part, tile_count[0].astype(F32)))
     hidden_grad = dot_nt(embed_grad, weights[2])
     sig = jax.nn.sigmoid(gate_proj)
     gate_grad = (hidden_grad * up_proj * sig * (1.0 + gate_proj * (1.0 - sig))).astype(BF16)
@@ -134,9 +432,15 @@
     partial = jnp.stack(
         (dot_tn(gate_grad, feats).astype(BF16), dot_tn(up_grad, feats).astype(BF16), dot_tn(hidden, embed_grad).astype(BF16))
     )
-    summed = lax.psum_scatter(partial, "col", scatter_dimension=1, tiled=True).astype(F32)
-    summed = summed * (0.5 * width ** -0.5 / totals[1])
-    entry_loss = totals[0] / (totals[1] * BLOCK * BLOCK)
+    summed = remote(
+        functools.partial(weight_kernel, col),
+        "weight",
+        3,
+        shaped((3, units, width), F32),
+        reduce_scratch(*col, (3, units, width)),
+    )(partial)
+    summed = summed * (0.5 * width ** -0.5 / totals[1, 0])
+    entry_loss = totals[0, 0] / (totals[1, 0] * BLOCK * BLOCK)
     return (entry_loss, summed[0].T, summed[1].T, summed[2])
 
 
@@ -153,4 +457,6 @@
         P(both),
     )
     out_specs = (P(), P(None, both), P(None, both), P(both, None))
-    return jax.shard_map(per_device, mesh=mesh, in_specs=in_specs, out_specs=out_specs, check_vma=False)
+    row = (mesh.shape["row"], 2)
+    col = (mesh.shape["col"], mesh.shape["col"] // 4)
+    return jax.shard_map(functools.partial(per_device, row, col), mesh=mesh, in_specs=in_specs, out_specs=out_specs, check_vma=False)

time: 402 us -> 174 us (0.43)
  waiting for transfers between devices: 292 us -> 0 us
  Pallas kernels: 28.4 us -> 158 us
  blocking collectives: 39.6 us -> 0 us
  between operations: 17.7 us -> 4.55 us
  other arithmetic: 8.16 us -> 1.21 us
  matrix products: 10.8 us -> 6.06 us
    all_gather x5 -> x0, waiting for transfers between devices: 148 us -> none  [the longest x1 51.1 us: per_device(): src_rows = lax.all_gather(embedding, 'col', axis=0, tiled=True)]
    reduce_scatter x4 -> x0, waiting for transfers between devices: 142 us -> none  [the longest x1 71.9 us: per_device(): lax.psum_scatter(src_part, 'col', scatter_dimension=0, tiled=True)]
    pallas_call x0 -> x4, Pallas kernels: none -> 131 us  [the longest x1 38.5 us: per_device(): remote(functools.partial(embed_kernel, row, col), 'embed', 1, (src_shape,...]
    psum x1 -> x0, blocking collectives: 39.6 us -> none  [per_device(): lax.psum(jnp.stack((loss_part[0, 0], tile_count[0].astype(F32))), ('row',...]
    dot_general x3, matrix products: 6.63 us -> 2.45 us  [dot_nt(): return lax.dot_general(a, b, NT, preferred_element_type=F32)]
  transfers between devices with their start and end apart: 9 -> 0, of which waited for: 9 -> 0; matrix products, arithmetic and copies ran while one was open for 1% -> 0% of each run, Pallas kernels for 0% -> 0%
where the time goes in v2:
time: 174 us
  Pallas kernels  158 us (91%)
  matrix products  6.06 us (3%)
  between operations  4.55 us (3%)
  local copies, waits for them, and re-layouts  3.82 us (2%)
    pallas_call x1, Pallas kernels, per_device(): remote(functools.partial(embed_kernel, row, col), 'embed', 1, (src_shape,...  38.5 us
    pallas_call x1, Pallas kernels, per_device(): remote(functools.partial(grad_kernel, row, col), 'grad', 2, (dst_shape, s...  37.2 us
    pallas_call x1, Pallas kernels, per_device(): remote(functools.partial(weight_kernel, col), 'weight', 3, shaped((3, uni...  28.6 us
    pallas_call x1, Pallas kernels, per_device(): remote(functools.partial(gather_in_kernel, row, col), 'gather_in', 0, (sh...  27 us
    pallas_call x1, Pallas kernels, tiles(): pl.pallas_call(functools.partial(tile_kernel, 0.5 * width ** (-0.5)), out...  26.8 us

profile of v2, /device:TPU:0, one launch (start us, length us, event | category | flops | bytes accessed | tf_op | source)
XLA Modules:
  0.0 173.6 jit_solution(330773813674547481)
XLA Ops:
  0.6 0.9 pad_maximum_fusion.1.w_ref
  1.6 0.0 copy-start.1
  1.6 0.9 copy-done.1
  2.5 27.0 %gather_in.1 = (bf16[3,512,512]{2,1,0:T(8,128)(2,1)S(1)}, bf16[1024,512]{1,0:T(8,128)(2,1)S(1)}) custom-call(bf16[3,64,512]{2,1,0:T(8,128)(2,1)S(1)} %pad_maximum_fusion.1.w_ref, bf16[256,512]{1,0:T(8,128)(2,1)S(1)} %copy-done.1), custom_call_target="tpu_custom_call" | custom-call | tf_op jit(solution)/shard_map/gather_in/pallas_call | solution.py:398
  29.5 0.7 fusion.8
  30.2 1.0 multiply_convert_fusion.2
  31.2 0.0 copy-start.2
  31.2 0.0 copy-start.3
  31.2 0.0 copy-start.4
  31.3 0.7 convolution_convert_fusion.branch_ref
  32.0 0.2 copy-done.2
  32.2 38.5 %embed.1 = (bf16[2048,512]{1,0:T(8,128)(2,1)S(1)}, bf16[1024,512]{1,0:T(8,128)(2,1)S(1)}) custom-call(bf16[1024,512]{1,0:T(8,128)(2,1)S(1)} %convolution_convert_fusion.branch_ref, bf16[256,512]{1,0:T(8,128)(2,1)S(1)} %copy-done.2), custom_call_target="tpu_custom_call" | custom-call | tf_op jit(solution)/shard_map/embed/pallas_call | solution.py:409
  70.7 0.0 copy-start
  70.7 1.3 copy-done
  72.6 0.0 copy-done.3
  72.7 0.0 copy-done.4
  72.7 26.8 %tiles.1 = (bf16[2048,512]{1,0:T(8,128)(2,1)S(1)}, bf16[1024,512]{1,0:T(8,128)(2,1)S(1)}, f32[8,128]{1,0:T(8,128)S(1)}) custom-call(s32[1]{0:T(128)S(6)} %copy.12.count_ref, s32[16]{0:T(128)S(1)} %copy-done.3, s32[16]{0:T(128)S(1)} %copy-done.4, bf16[2048,512]{1,0:T(8,128)(2,1)} %copy-done, bf16[1024,512]{1,0:T(8,128)(2,1)S(1)} %get-tuple-element.16.dst_ref, ...), custom_call_target="tpu_custom_call" | custom-call | tf_op jit(solution)/shard_map/tiles/pallas_call | solution.py:78
  99.4 0.1 broadcast_select_fusion.tot_ref
  99.5 37.2 %grad.1 = (bf16[1024,512]{1,0:T(8,128)(2,1)S(1)}, f32[8,128]{1,0:T(8,128)S(1)}) custom-call(bf16[2048,512]{1,0:T(8,128)(2,1)S(1)} %get-tuple-element.17.src_ref, bf16[1024,512]{1,0:T(8,128)(2,1)S(1)} %get-tuple-element.18.dst_ref, f32[8,128]{1,0:T(8,128)S(1)} %broadcast_select_fusion.tot_ref), custom_call_target="tpu_custom_call" | custom-call | tf_op jit(solution)/shard_map/grad/pallas_call | solution.py:419
  136.7 0.7 fusion.3
  137.5 1.3 fusion
  138.8 0.8 fusion.1
  139.7 0.7 fusion.2
  140.4 0.2 pad_maximum_fusion.part_ref
  140.6 28.6 %weight.1 = f32[3,64,512]{2,1,0:T(8,128)S(1)} custom-call(bf16[3,512,512]{2,1,0:T(8,128)(2,1)S(1)} %pad_maximum_fusion.part_ref), custom_call_target="tpu_custom_call" | custom-call | tf_op jit(solution)/shard_map/weight/pallas_call | solution.py:435
  169.2 0.6 fusion.16
  170.5 0.8 slice_bitcast_fusion
  (2 shorter events, 0.0 us)
Async XLA Ops:
  1.6 1.0 copy-start.1
  31.2 1.0 copy-start.2
  31.2 41.4 %copy-start.3 = (s32[16]{0:T(128)S(1)}, s32[16]{0:T(128)}, u32[]{:S(2)}) copy-start(s32[16]{0:T(128)} %src_id.1) | copy-start | bytes 196
  31.2 41.4 %copy-start.4 = (s32[16]{0:T(128)S(1)}, s32[16]{0:T(128)}, u32[]{:S(2)}) copy-start(s32[16]{0:T(128)} %dst_id.1) | copy-start | bytes 196
  70.7 1.3 copy-start

commit v3 on v2

--- a/solution.py
+++ b/solution.py
@@ -9,6 +9,7 @@
 from jax.sharding import PartitionSpec as P
 
 BLOCK = 512
+CHUNKS = 4
 F32 = jnp.float32
 BF16 = jnp.bfloat16
 NT = (((1,), (1,)), ((), ()))
@@ -108,10 +109,28 @@
     )(tile_count, tile_src, tile_dst, src_rows, dst_rows, tile_mask)
 
 
-def finish(steps):
-    steps = list(steps)
+def advance(steps):
+    return [step for step in steps if next(step, True) is None]
+
+
+def together(*steps):
+    steps = advance(steps)
     while steps:
-        steps = [step for step in steps if next(step, True) is None]
+        yield
+        steps = advance(steps)
+
+
+def finish(*steps):
+    for _ in together(*steps):
+        pass
+
+
+def wavefront(steps):
+    waiting = advance(steps)
+    running = []
+    while waiting or running:
+        running = advance(waiting[:1] + running)
+        waiting = waiting[1:]
 
 
 def group(axis, n, inner):
@@ -251,7 +270,7 @@
         if off:
             out[off - 1] = total.astype(BF16)
             along(off).start()
-            yield
+    yield
     for off in order[:-1]:
         along(off).wait_recv()
         total = total + far[off - 1].astype(F32)
@@ -318,60 +337,95 @@
     pl.semaphore_wait(barrier, total)
 
 
-def rows_of(ref, size):
-    return lambda block: ref.at[pl.ds(pl.multiple_of(block * size, size), size), :]
-
-
-def units_of(ref, size):
-    return lambda block: ref.at[:, pl.ds(pl.multiple_of(block * size, size), size), :]
-
-
-def gather_in_kernel(row, col, w_ref, x_ref, w_out, x_out, *sems):
+def rows_of(ref, size, part, chunk):
+    return lambda block: ref.at[pl.ds(pl.multiple_of(block * size + chunk * part, part), part), :]
+
+
+def units_of(ref, size, kind):
+    return lambda block: ref.at[kind, pl.ds(pl.multiple_of(block * size, size), size), :]
+
+
+def rows(ref, part, chunk):
+    return ref.at[pl.ds(chunk * part, part), :]
+
+
+def take(scratch, count):
+    taken = scratch[:count]
+    del scratch[:count]
+    return taken
+
+
+def gather_in_kernel(row, col, w_ref, x_ref, w_out, x_out, *scratch):
     greet((("row", row[0]), ("col", col[0])))
-    finish((
-        gather("col", *col, w_ref, units_of(w_out, w_ref.shape[1]), *sems[:2]),
-        gather("row", *row, x_ref, rows_of(x_out, x_ref.shape[0]), *sems[2:]),
-    ))
-
-
-def embed_kernel(row, col, branch_ref, x_ref, src_out, dst_out, held, *scratch):
+    scratch = list(scratch)
+    kinds, units = w_ref.shape[:2]
+    size = x_ref.shape[0]
+    steps = [
+        gather("col", *col, w_ref.at[kind], units_of(w_out, units, kind), *take(scratch, 2)) for kind in range(kinds)
+    ]
+    steps.append(gather("row", *row, x_ref, rows_of(x_out, size, size, 0), *take(scratch, 2)))
+    finish(*steps)
+
+
+def embed_kernel(row, col, chunks, branch_ref, x_ref, src_out, dst_out, held, *scratch):
     greet((("row", row[0]), ("col", col[0])))
+    scratch = list(scratch)
     size = x_ref.shape[0]
-    branch = []
-    finish((reduce("row", *row, rows_of(branch_ref, size), *scratch[:5], branch),))
-    held[...] = (x_ref[...].astype(F32) + branch[0]).astype(BF16)
-    finish((
-        gather("col", *col, held, rows_of(src_out, size), *scratch[5:7]),
-        gather("row", *row, held, rows_of(dst_out, size), *scratch[7:9]),
-    ))
-
-
-def grad_kernel(row, col, src_ref, dst_ref, tot_ref, grad_out, tot_out, held, tot_held, *scratch):
+    part = size // chunks
+
+    def chain(chunk, sum_refs, col_sems, row_sems):
+        branch = []
+        yield from reduce("row", *row, rows_of(branch_ref, size, part, chunk), *sum_refs, branch)
+        own = rows(held, part, chunk)
+        own[...] = (rows(x_ref, part, chunk)[...].astype(F32) + branch[0]).astype(BF16)
+        yield from together(
+            gather("col", *col, own, rows_of(src_out, size, part, chunk), *col_sems),
+            gather("row", *row, own, rows_of(dst_out, size, part, chunk), *row_sems),
+        )
+
+    wavefront([chain(chunk, take(scratch, 5), take(scratch, 2), take(scratch, 2)) for chunk in range(chunks)])
+
+
+def grad_kernel(row, col, chunks, src_ref, dst_ref, tot_ref, grad_out, tot_out, held, tot_held, *scratch):
     greet((("row", row[0]), ("col", col[0])))
+    scratch = list(scratch)
     size = held.shape[0]
-    own, first, second = [], [], []
-
-    def totals():
-        yield from sum_over("row", row[0], tot_ref, *scratch[12:15], first)
+    part = size // chunks
+
+    def totals(row_refs, col_refs):
+        first, second = [], []
+        yield from sum_over("row", row[0], tot_ref, *row_refs, first)
         tot_held[...] = first[0]
         yield
-        yield from sum_over("col", col[0], tot_held, *scratch[15:18], second)
+        yield from sum_over("col", col[0], tot_held, *col_refs, second)
         tot_out[...] = second[0]
 
-    finish((
-        reduce("col", *col, rows_of(src_ref, size), *scratch[:5], own),
-        reduce("row", *row, rows_of(dst_ref, size), *scratch[5:10], own),
-        totals(),
-    ))
-    held[...] = (own[0] + own[1]).astype(BF16)
-    finish((gather("row", *row, held, rows_of(grad_out, size), *scratch[10:12]),))
+    def chain(chunk, col_refs, row_refs, row_sems):
+        total = []
+        yield from together(
+            reduce("row", *row, rows_of(dst_ref, size, part, chunk), *row_refs, total),
+            reduce("col", *col, rows_of(src_ref, size, part, chunk), *col_refs, total),
+        )
+        own = rows(held, part, chunk)
+        own[...] = (total[0] + total[1]).astype(BF16)
+        yield from gather("row", *row, own, rows_of(grad_out, size, part, chunk), *row_sems)
+
+    steps = [totals(take(scratch, 3), take(scratch, 3))]
+    steps += [chain(chunk, take(scratch, 5), take(scratch, 5), take(scratch, 2)) for chunk in range(chunks)]
+    wavefront(steps)
 
 
 def weight_kernel(col, part_ref, sum_out, *scratch):
     greet((("col", col[0]),))
-    total = []
-    finish((reduce("col", *col, units_of(part_ref, sum_out.shape[1]), *scratch, total),))
-    sum_out[...] = total[0]
+    scratch = list(scratch)
+    kinds, units = sum_out.shape[:2]
+
+    def chain(kind, refs):
+        total = []
+        yield from reduce("col", *col, units_of(part_ref, units, kind), *refs, total)
+        sum_out[kind] = total[0]
+
+    wavefront([chain(kind, take(scratch, 5)) for kind in range(kinds)])
 
 
 def remote(kernel, name, number, outs, scratch):
@@ -400,30 +454,34 @@
         "gather_in",
         0,
         (shaped((3, col[0] * units, width), BF16), dst_shape),
-        gather_sems(*col) + gather_sems(*row),
+        gather_sems(*col) * 3 + gather_sems(*row),
     )(stacked, node_feats)
     gate_proj = dot_nt(feats, weights[0])
     up_proj = dot_nt(feats, weights[1])
     hidden = (jax.nn.silu(gate_proj) * up_proj).astype(BF16)
     branch = jnp.dot(hidden, weights[2], preferred_element_type=F32).astype(BF16)
     src_rows, dst_rows = remote(
-        functools.partial(embed_kernel, row, col),
+        functools.partial(embed_kernel, row, col, CHUNKS),
         "embed",
         1,
         (src_shape, dst_shape),
         [pltpu.VMEM((size, width), BF16)]
-        + reduce_scratch(*row, (size, width)) + gather_sems(*col) + gather_sems(*row),
+        + (reduce_scratch(*row, (size // CHUNKS, width)) + gather_sems(*col) + gather_sems(*row)) * CHUNKS,
     )(branch, node_feats)
     src_part, dst_part, loss_part = tiles(src_rows, dst_rows, tile_src, tile_dst, tile_mask, tile_count)
     is_loss = lax.broadcasted_iota(jnp.int32, loss_part.shape, 0) == 0
     embed_grad, totals = remote(
-        functools.partial(grad_kernel, row, col),
+        functools.partial(grad_kernel, row, col, CHUNKS),
         "grad",
         2,
         (dst_shape, shaped(loss_part.shape, F32)),
         [pltpu.VMEM((size, width), BF16), pltpu.VMEM(loss_part.shape, F32)]
-        + reduce_scratch(*col, (size, width)) + reduce_scratch(*row, (size, width)) + gather_sems(*row)
-        + sum_scratch(row[0]) + sum_scratch(col[0]),
+        + sum_scratch(row[0]) + sum_scratch(col[0])
+        + (
+            reduce_scratch(*col, (size // CHUNKS, width))
+            + reduce_scratch(*row, (size // CHUNKS, width))
+            + gather_sems(*row)
+        ) * CHUNKS,
     )(src_part, dst_part, jnp.where(is_loss, loss_part, tile_count[0].astype(F32)))
     hidden_grad = dot_nt(embed_grad, weights[2])
     sig = jax.nn.sigmoid(gate_proj)
@@ -437,7 +495,7 @@
         "weight",
         3,
         shaped((3, units, width), F32),
-        reduce_scratch(*col, (3, units, width)),
+        reduce_scratch(*col, (units, width)) * 3,
     )(partial)
     summed = summed * (0.5 * width ** -0.5 / totals[1, 0])
     entry_loss = totals[0, 0] / (totals[1, 0] * BLOCK * BLOCK)

time: 174 us -> 167 us (0.960)
  Pallas kernels: 158 us -> 152 us
    pallas_call x1, Pallas kernels: 28.6 us -> 24.6 us  [per_device(): remote(functools.partial(weight_kernel, col), 'weight', 3, shaped((3, uni...]
    pallas_call x1, Pallas kernels: 27 us -> 24.6 us  [per_device(): remote(functools.partial(gather_in_kernel, row, col), 'gather_in', 0, (sh...]
where the time goes in v3:
time: 167 us; the launch traced here: 168 us
  Pallas kernels  152 us (91%)
  matrix products  6.06 us (4%)
  between operations  4.55 us (3%)
  local copies, waits for them, and re-layouts  3.82 us (2%)
    pallas_call x1, Pallas kernels, per_device(): remote(functools.partial(grad_kernel, row, col, CHUNKS), 'grad', 2, (dst_...  42.3 us
    pallas_call x1, Pallas kernels, per_device(): remote(functools.partial(embed_kernel, row, col, CHUNKS), 'embed', 1, (sr...  33.6 us
    pallas_call x1, Pallas kernels, tiles(): pl.pallas_call(functools.partial(tile_kernel, 0.5 * width ** (-0.5)), out...  26.8 us
    pallas_call x1, Pallas kernels, per_device(): remote(functools.partial(weight_kernel, col), 'weight', 3, shaped((3, uni...  24.6 us
    pallas_call x1, Pallas kernels, per_device(): remote(functools.partial(gather_in_kernel, row, col), 'gather_in', 0, (sh...  24.6 us

profile of v3, /device:TPU:0, one launch (start us, length us, event | category | flops | bytes accessed | tf_op | source)
XLA Modules:
  0.0 167.5 jit_solution(3357140136829163368)
XLA Ops:
  0.6 0.9 pad_maximum_fusion.1.w_ref
  1.6 0.0 copy-start.1
  1.6 0.9 copy-done.1
  2.5 24.6 %gather_in.1 = (bf16[3,512,512]{2,1,0:T(8,128)(2,1)S(1)}, bf16[1024,512]{1,0:T(8,128)(2,1)S(1)}) custom-call(bf16[3,64,512]{2,1,0:T(8,128)(2,1)S(1)} %pad_maximum_fusion.1.w_ref, bf16[256,512]{1,0:T(8,128)(2,1)S(1)} %copy-done.1), custom_call_target="tpu_custom_call" | custom-call | tf_op jit(solution)/shard_map/gather_in/pallas_call | solution.py:452
  27.1 0.7 fusion.8
  27.9 1.0 multiply_convert_fusion.2
  28.9 0.0 copy-start.2
  28.9 0.0 copy-start.3
  28.9 0.0 copy-start.4
  28.9 0.7 convolution_convert_fusion.branch_ref
  29.6 0.2 copy-done.2
  29.8 33.6 %embed.1 = (bf16[2048,512]{1,0:T(8,128)(2,1)S(1)}, bf16[1024,512]{1,0:T(8,128)(2,1)S(1)}) custom-call(bf16[1024,512]{1,0:T(8,128)(2,1)S(1)} %convolution_convert_fusion.branch_ref, bf16[256,512]{1,0:T(8,128)(2,1)S(1)} %copy-done.2), custom_call_target="tpu_custom_call" | custom-call | tf_op jit(solution)/shard_map/embed/pallas_call | solution.py:463
  63.4 0.0 copy-start
  63.5 1.3 copy-done
  65.4 0.0 copy-done.3
  65.4 0.0 copy-done.4
  65.4 26.8 %tiles.1 = (bf16[2048,512]{1,0:T(8,128)(2,1)S(1)}, bf16[1024,512]{1,0:T(8,128)(2,1)S(1)}, f32[8,128]{1,0:T(8,128)S(1)}) custom-call(s32[1]{0:T(128)S(6)} %copy.12.count_ref, s32[16]{0:T(128)S(1)} %copy-done.3, s32[16]{0:T(128)S(1)} %copy-done.4, bf16[2048,512]{1,0:T(8,128)(2,1)} %copy-done, bf16[1024,512]{1,0:T(8,128)(2,1)S(1)} %get-tuple-element.16.dst_ref, ...), custom_call_target="tpu_custom_call" | custom-call | tf_op jit(solution)/shard_map/tiles/pallas_call | solution.py:79
  92.2 0.1 broadcast_select_fusion.tot_ref
  92.3 42.3 %grad.1 = (bf16[1024,512]{1,0:T(8,128)(2,1)S(1)}, f32[8,128]{1,0:T(8,128)S(1)}) custom-call(bf16[2048,512]{1,0:T(8,128)(2,1)S(1)} %get-tuple-element.17.src_ref, bf16[1024,512]{1,0:T(8,128)(2,1)S(1)} %get-tuple-element.18.dst_ref, f32[8,128]{1,0:T(8,128)S(1)} %broadcast_select_fusion.tot_ref), custom_call_target="tpu_custom_call" | custom-call | tf_op jit(solution)/shard_map/grad/pallas_call | solution.py:473
  134.6 0.7 fusion.3
  135.3 1.3 fusion
  136.7 0.8 fusion.1
  137.5 0.7 fusion.2
  138.2 0.2 pad_maximum_fusion.part_ref
  138.4 24.6 %weight.1 = f32[3,64,512]{2,1,0:T(8,128)S(1)} custom-call(bf16[3,512,512]{2,1,0:T(8,128)(2,1)S(1)} %pad_maximum_fusion.part_ref), custom_call_target="tpu_custom_call" | custom-call | tf_op jit(solution)/shard_map/weight/pallas_call | solution.py:493
  163.1 0.6 fusion.16
  164.4 0.8 slice_bitcast_fusion
  (2 shorter events, 0.0 us)
Async XLA Ops:
  1.6 1.0 copy-start.1
  28.9 1.0 copy-start.2
  28.9 36.6 %copy-start.3 = (s32[16]{0:T(128)S(1)}, s32[16]{0:T(128)}, u32[]{:S(2)}) copy-start(s32[16]{0:T(128)} %src_id.1) | copy-start | bytes 196
  28.9 36.6 %copy-start.4 = (s32[16]{0:T(128)S(1)}, s32[16]{0:T(128)}, u32[]{:S(2)}) copy-start(s32[16]{0:T(128)} %dst_id.1) | copy-start | bytes 196
  63.4 1.3 copy-start

commit v4 on v3

--- a/solution.py
+++ b/solution.py
@@ -232,7 +232,7 @@
     return [pltpu.SemaphoreType.DMA((count,)), pltpu.SemaphoreType.DMA((count,))]
 
 
-def reduce(axis, n, inner, place, near, out, far, send, recv, result):
+def reduce(axis, n, inner, place, near, out, far, send, recv, result, fine=False):
     outer = n // inner
     me, at_o, at_i = group(axis, n, inner)
     order = sorted(range(outer), key=lambda off: -min(off, outer - off))
@@ -261,7 +261,10 @@
     for off in order:
         for j in range(1, inner):
             across(j, off).start()
-    yield
+        if fine:
+            yield
+    if not fine:
+        yield
     for off in order:
         total = place(lax.rem(at_o + off, outer) * inner + at_i)[...].astype(F32)
         for j in range(1, inner):
@@ -270,7 +273,10 @@
         if off:
             out[off - 1] = total.astype(BF16)
             along(off).start()
-    yield
+        if fine:
+            yield
+    if not fine:
+        yield
     for off in order[:-1]:
         along(off).wait_recv()
         total = total + far[off - 1].astype(F32)
@@ -404,7 +410,7 @@
         total = []
         yield from together(
             reduce("row", *row, rows_of(dst_ref, size, part, chunk), *row_refs, total),
-            reduce("col", *col, rows_of(src_ref, size, part, chunk), *col_refs, total),
+            reduce("col", *col, rows_of(src_ref, size, part, chunk), *col_refs, total, True),
         )
         own = rows(held, part, chunk)
         own[...] = (total[0] + total[1]).astype(BF16)
@@ -412,7 +418,7 @@
 
     steps = [totals(take(scratch, 3), take(scratch, 3))]
     steps += [chain(chunk, take(scratch, 5), take(scratch, 5), take(scratch, 2)) for chunk in range(chunks)]
-    wavefront(steps)
+    finish(*steps)
 
 
 def weight_kernel(col, part_ref, sum_out, *scratch):
@@ -422,10 +428,10 @@
 
     def chain(kind, refs):
         total = []
-        yield from reduce("col", *col, units_of(part_ref, units, kind), *refs, total)
+        yield from reduce("col", *col, units_of(part_ref, units, kind), *refs, total, True)
         sum_out[kind] = total[0]
 
-    wavefront([chain(kind, take(scratch, 5)) for kind in range(kinds)])
+    finish(*[chain(kind, take(scratch, 5)) for kind in range(kinds)])
 
 
 def remote(kernel, name, number, outs, scratch):

time: 167 us -> 168 us (level)
    pallas_call x1, Pallas kernels: 42.3 us -> 38 us  [per_device(): remote(functools.partial(grad_kernel, row, col, CHUNKS), 'grad', 2, (dst_...]
    pallas_call x1, Pallas kernels: 24.6 us -> 28.6 us  [per_device(): remote(functools.partial(weight_kernel, col), 'weight', 3, shaped((3, uni...]
where the time goes in v4:
time: 168 us; the launch traced here: 167 us
  Pallas kernels  152 us (90%)
  matrix products  6.05 us (4%)
  between operations  4.55 us (3%)
  local copies, waits for them, and re-layouts  3.82 us (2%)
    pallas_call x1, Pallas kernels, per_device(): remote(functools.partial(grad_kernel, row, col, CHUNKS), 'grad', 2, (dst_...  38 us
    pallas_call x1, Pallas kernels, per_device(): remote(functools.partial(embed_kernel, row, col, CHUNKS), 'embed', 1, (sr...  33.6 us
    pallas_call x1, Pallas kernels, per_device(): remote(functools.partial(weight_kernel, col), 'weight', 3, shaped((3, uni...  28.6 us
    pallas_call x1, Pallas kernels, tiles(): pl.pallas_call(functools.partial(tile_kernel, 0.5 * width ** (-0.5)), out...  26.8 us
    pallas_call x1, Pallas kernels, per_device(): remote(functools.partial(gather_in_kernel, row, col), 'gather_in', 0, (sh...  24.6 us

profile of v4, /device:TPU:0, one launch (start us, length us, event | category | flops | bytes accessed | tf_op | source)
XLA Modules:
  0.0 167.2 jit_solution(596221038167801124)
XLA Ops:
  0.6 0.9 pad_maximum_fusion.1.w_ref
  1.6 0.0 copy-start.1
  1.6 0.9 copy-done.1
  2.5 24.6 %gather_in.1 = (bf16[3,512,512]{2,1,0:T(8,128)(2,1)S(1)}, bf16[1024,512]{1,0:T(8,128)(2,1)S(1)}) custom-call(bf16[3,64,512]{2,1,0:T(8,128)(2,1)S(1)} %pad_maximum_fusion.1.w_ref, bf16[256,512]{1,0:T(8,128)(2,1)S(1)} %copy-done.1), custom_call_target="tpu_custom_call" | custom-call | tf_op jit(solution)/shard_map/gather_in/pallas_call | solution.py:458
  27.1 0.7 fusion.8
  27.9 1.0 multiply_convert_fusion.2
  28.9 0.0 copy-start.2
  28.9 0.0 copy-start.3
  28.9 0.0 copy-start.4
  28.9 0.7 convolution_convert_fusion.branch_ref
  29.6 0.2 copy-done.2
  29.8 33.6 %embed.1 = (bf16[2048,512]{1,0:T(8,128)(2,1)S(1)}, bf16[1024,512]{1,0:T(8,128)(2,1)S(1)}) custom-call(bf16[1024,512]{1,0:T(8,128)(2,1)S(1)} %convolution_convert_fusion.branch_ref, bf16[256,512]{1,0:T(8,128)(2,1)S(1)} %copy-done.2), custom_call_target="tpu_custom_call" | custom-call | tf_op jit(solution)/shard_map/embed/pallas_call | solution.py:469
  63.4 0.0 copy-start
  63.5 1.3 copy-done
  65.4 0.0 copy-done.3
  65.4 0.0 copy-done.4
  65.4 26.8 %tiles.1 = (bf16[2048,512]{1,0:T(8,128)(2,1)S(1)}, bf16[1024,512]{1,0:T(8,128)(2,1)S(1)}, f32[8,128]{1,0:T(8,128)S(1)}) custom-call(s32[1]{0:T(128)S(6)} %copy.12.count_ref, s32[16]{0:T(128)S(1)} %copy-done.3, s32[16]{0:T(128)S(1)} %copy-done.4, bf16[2048,512]{1,0:T(8,128)(2,1)} %copy-done, bf16[1024,512]{1,0:T(8,128)(2,1)S(1)} %get-tuple-element.16.dst_ref, ...), custom_call_target="tpu_custom_call" | custom-call | tf_op jit(solution)/shard_map/tiles/pallas_call | solution.py:79
  92.2 0.1 broadcast_select_fusion.tot_ref
  92.3 38.0 %grad.1 = (bf16[1024,512]{1,0:T(8,128)(2,1)S(1)}, f32[8,128]{1,0:T(8,128)S(1)}) custom-call(bf16[2048,512]{1,0:T(8,128)(2,1)S(1)} %get-tuple-element.17.src_ref, bf16[1024,512]{1,0:T(8,128)(2,1)S(1)} %get-tuple-element.18.dst_ref, f32[8,128]{1,0:T(8,128)S(1)} %broadcast_select_fusion.tot_ref), custom_call_target="tpu_custom_call" | custom-call | tf_op jit(solution)/shard_map/grad/pallas_call | solution.py:479
  130.3 0.7 fusion.3
  131.0 1.3 fusion
  132.4 0.8 fusion.1
  133.2 0.7 fusion.2
  134.0 0.2 pad_maximum_fusion.part_ref
  134.1 28.6 %weight.1 = f32[3,64,512]{2,1,0:T(8,128)S(1)} custom-call(bf16[3,512,512]{2,1,0:T(8,128)(2,1)S(1)} %pad_maximum_fusion.part_ref), custom_call_target="tpu_custom_call" | custom-call | tf_op jit(solution)/shard_map/weight/pallas_call | solution.py:499
  162.7 0.6 fusion.16
  164.0 0.8 slice_bitcast_fusion
  (2 shorter events, 0.0 us)
Async XLA Ops:
  1.6 1.0 copy-start.1
  28.9 1.0 copy-start.2
  28.9 36.6 %copy-start.3 = (s32[16]{0:T(128)S(1)}, s32[16]{0:T(128)}, u32[]{:S(2)}) copy-start(s32[16]{0:T(128)} %src_id.1) | copy-start | bytes 196
  28.9 36.6 %copy-start.4 = (s32[16]{0:T(128)S(1)}, s32[16]{0:T(128)}, u32[]{:S(2)}) copy-start(s32[16]{0:T(128)} %dst_id.1) | copy-start | bytes 196
  63.4 1.3 copy-start

commit v5 on v4

--- a/solution.py
+++ b/solution.py
@@ -10,6 +10,7 @@
 
 BLOCK = 512
 CHUNKS = 4
+GRAD_CHUNKS = 2
 F32 = jnp.float32
 BF16 = jnp.bfloat16
 NT = (((1,), (1,)), ((), ()))
@@ -428,10 +429,10 @@
 
     def chain(kind, refs):
         total = []
-        yield from reduce("col", *col, units_of(part_ref, units, kind), *refs, total, True)
+        yield from reduce("col", *col, units_of(part_ref, units, kind), *refs, total)
         sum_out[kind] = total[0]
 
-    finish(*[chain(kind, take(scratch, 5)) for kind in range(kinds)])
+    wavefront([chain(kind, take(scratch, 5)) for kind in range(kinds)])
 
 
 def remote(kernel, name, number, outs, scratch):
@@ -477,17 +478,17 @@
     src_part, dst_part, loss_part = tiles(src_rows, dst_rows, tile_src, tile_dst, tile_mask, tile_count)
     is_loss = lax.broadcasted_iota(jnp.int32, loss_part.shape, 0) == 0
     embed_grad, totals = remote(
-        functools.partial(grad_kernel, row, col, CHUNKS),
+        functools.partial(grad_kernel, row, col, GRAD_CHUNKS),
         "grad",
         2,
         (dst_shape, shaped(loss_part.shape, F32)),
         [pltpu.VMEM((size, width), BF16), pltpu.VMEM(loss_part.shape, F32)]
         + sum_scratch(row[0]) + sum_scratch(col[0])
         + (
-            reduce_scratch(*col, (size // CHUNKS, width))
-            + reduce_scratch(*row, (size // CHUNKS, width))
+            reduce_scratch(*col, (size // GRAD_CHUNKS, width))
+            + reduce_scratch(*row, (size // GRAD_CHUNKS, width))
             + gather_sems(*row)
-        ) * CHUNKS,
+        ) * GRAD_CHUNKS,
     )(src_part, dst_part, jnp.where(is_loss, loss_part, tile_count[0].astype(F32)))
     hidden_grad = dot_nt(embed_grad, weights[2])
     sig = jax.nn.sigmoid(gate_proj)

time: 168 us -> 168 us (level)
    pallas_call x1, Pallas kernels: 38 us -> 40.4 us  [per_device(): remote(functools.partial(grad_kernel, row, col, GRAD_CHUNKS), 'grad', 2,...]
where the time goes in v5:
time: 168 us
  Pallas kernels  153 us (91%)
  matrix products  6.05 us (4%)
  between operations  4.55 us (3%)
  local copies, waits for them, and re-layouts  3.82 us (2%)
    pallas_call x1, Pallas kernels, per_device(): remote(functools.partial(grad_kernel, row, col, GRAD_CHUNKS), 'grad', 2,...  40.4 us
    pallas_call x1, Pallas kernels, per_device(): remote(functools.partial(embed_kernel, row, col, CHUNKS), 'embed', 1, (sr...  33.6 us
    pallas_call x1, Pallas kernels, per_device(): remote(functools.partial(weight_kernel, col), 'weight', 3, shaped((3, uni...  27.3 us
    pallas_call x1, Pallas kernels, tiles(): pl.pallas_call(functools.partial(tile_kernel, 0.5 * width ** (-0.5)), out...  26.8 us
    pallas_call x1, Pallas kernels, per_device(): remote(functools.partial(gather_in_kernel, row, col), 'gather_in', 0, (sh...  24.6 us

profile of v5, /device:TPU:0, one launch (start us, length us, event | category | flops | bytes accessed | tf_op | source)
XLA Modules:
  0.0 168.4 jit_solution(1891210370742239732)
XLA Ops:
  0.6 0.9 pad_maximum_fusion.1.w_ref
  1.6 0.0 copy-start.1
  1.6 0.9 copy-done.1
  2.5 24.6 %gather_in.1 = (bf16[3,512,512]{2,1,0:T(8,128)(2,1)S(1)}, bf16[1024,512]{1,0:T(8,128)(2,1)S(1)}) custom-call(bf16[3,64,512]{2,1,0:T(8,128)(2,1)S(1)} %pad_maximum_fusion.1.w_ref, bf16[256,512]{1,0:T(8,128)(2,1)S(1)} %copy-done.1), custom_call_target="tpu_custom_call" | custom-call | tf_op jit(solution)/shard_map/gather_in/pallas_call | solution.py:459
  27.1 0.7 fusion.8
  27.9 1.0 multiply_convert_fusion.2
  28.9 0.0 copy-start.2
  28.9 0.0 copy-start.3
  28.9 0.0 copy-start.4
  28.9 0.7 convolution_convert_fusion.branch_ref
  29.6 0.2 copy-done.2
  29.8 33.6 %embed.1 = (bf16[2048,512]{1,0:T(8,128)(2,1)S(1)}, bf16[1024,512]{1,0:T(8,128)(2,1)S(1)}) custom-call(bf16[1024,512]{1,0:T(8,128)(2,1)S(1)} %convolution_convert_fusion.branch_ref, bf16[256,512]{1,0:T(8,128)(2,1)S(1)} %copy-done.2), custom_call_target="tpu_custom_call" | custom-call | tf_op jit(solution)/shard_map/embed/pallas_call | solution.py:470
  63.4 0.0 copy-start
  63.5 1.3 copy-done
  65.4 0.0 copy-done.3
  65.4 0.0 copy-done.4
  65.4 26.8 %tiles.1 = (bf16[2048,512]{1,0:T(8,128)(2,1)S(1)}, bf16[1024,512]{1,0:T(8,128)(2,1)S(1)}, f32[8,128]{1,0:T(8,128)S(1)}) custom-call(s32[1]{0:T(128)S(6)} %copy.12.count_ref, s32[16]{0:T(128)S(1)} %copy-done.3, s32[16]{0:T(128)S(1)} %copy-done.4, bf16[2048,512]{1,0:T(8,128)(2,1)} %copy-done, bf16[1024,512]{1,0:T(8,128)(2,1)S(1)} %get-tuple-element.16.dst_ref, ...), custom_call_target="tpu_custom_call" | custom-call | tf_op jit(solution)/shard_map/tiles/pallas_call | solution.py:80
  92.2 0.1 broadcast_select_fusion.tot_ref
  92.3 40.4 %grad.1 = (bf16[1024,512]{1,0:T(8,128)(2,1)S(1)}, f32[8,128]{1,0:T(8,128)S(1)}) custom-call(bf16[2048,512]{1,0:T(8,128)(2,1)S(1)} %get-tuple-element.17.src_ref, bf16[1024,512]{1,0:T(8,128)(2,1)S(1)} %get-tuple-element.18.dst_ref, f32[8,128]{1,0:T(8,128)S(1)} %broadcast_select_fusion.tot_ref), custom_call_target="tpu_custom_call" | custom-call | tf_op jit(solution)/shard_map/grad/pallas_call | solution.py:480
  132.7 0.7 fusion.3
  133.5 1.3 fusion
  134.8 0.8 fusion.1
  135.7 0.7 fusion.2
  136.4 0.2 pad_maximum_fusion.part_ref
  136.6 27.3 %weight.1 = f32[3,64,512]{2,1,0:T(8,128)S(1)} custom-call(bf16[3,512,512]{2,1,0:T(8,128)(2,1)S(1)} %pad_maximum_fusion.part_ref), custom_call_target="tpu_custom_call" | custom-call | tf_op jit(solution)/shard_map/weight/pallas_call | solution.py:500
  163.9 0.6 fusion.16
  165.2 0.8 slice_bitcast_fusion
  (2 shorter events, 0.0 us)
Async XLA Ops:
  1.6 1.0 copy-start.1
  28.9 1.0 copy-start.2
  28.9 36.6 %copy-start.3 = (s32[16]{0:T(128)S(1)}, s32[16]{0:T(128)}, u32[]{:S(2)}) copy-start(s32[16]{0:T(128)} %src_id.1) | copy-start | bytes 196
  28.9 36.6 %copy-start.4 = (s32[16]{0:T(128)S(1)}, s32[16]{0:T(128)}, u32[]{:S(2)}) copy-start(s32[16]{0:T(128)} %dst_id.1) | copy-start | bytes 196
  63.4 1.3 copy-start
